TPU v7x, 128 devices: a whole 4x4x4 slice. The times are simulated.
128 devices in a mesh: heads: 4 (over y_lo, core), seq: 32 (over z, y_hi, x).
Axes of the slice: x: 4, y: 4 (y_hi: 2, y_lo: 2; y = y_hi * 2 + y_lo), z: 4, core: 2. Of those that a mesh axis runs over, the one named last changes fastest.
Arguments:
- queries: bfloat16 [16384, 4096], P('seq', 'heads'), may hold values from -6 to 6
- keys: bfloat16 [16384, 1024], P('seq', 'heads'), may hold values from -6 to 6
- values: bfloat16 [16384, 1024], P('seq', 'heads'), may hold values from -6 to 6
- out: bfloat16 [16384, 4096], P('seq', 'heads'), may hold values from -1.796875 to 1.796875
- output_gradient: bfloat16 [16384, 4096], P('seq', 'heads'), may hold values from -384 to 384
- lse: float32 [32, 16384], P('heads', 'seq'), may hold values from 0 to 20, as said below
Outputs:
- d_queries: bfloat16 [16384, 4096], P('seq', 'heads')
- key_gradient: bfloat16 [16384, 1024], P('seq', 'heads')
- value_gradient: bfloat16 [16384, 1024], P('seq', 'heads')
Inputs may be any that keep to these rules, and one draw needn't show every extreme that they name: `lse`: positive and finite; one entry for each query head and position.
All inputs are finite; a program needn't handle non-finite values.
Results may differ from a plain program's by a relative error of at most 0.0054.
Values may be sent and summed in bfloat16 or wider, within the bound.
A program may use at most 128 MiB of HBM per device.

v0:
```python
import functools

import jax
import jax.numpy as jnp
from jax import lax
from jax.experimental import pallas as pl
from jax.experimental.pallas import tpu as pltpu
from jax.sharding import PartitionSpec as P

HEAD = 128
GROUP = 4
TOK = 512
SCALE = HEAD ** (-0.5)
LOG2E = 1.4426950408889634
f32, bf16 = jnp.float32, jnp.bfloat16
NT = (((1,), (1,)), ((), ()))
NN = (((1,), (0,)), ((), ()))
TN = (((0,), (0,)), ((), ()))

BACK = (0, 2, 4, 1, 3)
ITEMS = (
    (0, 0, 0), (0, 0, 1), (0, 1, 0), (0, 2, 0), (0, 1, 1), (0, 2, 1),
    (0, 3, 1), (0, 3, 0), (0, 4, 1), (0, 4, 0),
    (1, 3, 1), (1, 3, 0), (1, 4, 1), (1, 4, 0),
    (1, 1, 0), (1, 1, 1), (1, 2, 0), (1, 2, 1), (1, 0, 1), (1, 0, 0),
)


def dot(a, b, dims):
    return lax.dot_general(a, b, dims, preferred_element_type=f32)


def pick(i, values):
    out = jnp.int32(values[0])
    for j, v in enumerate(values):
        if j:
            out = jnp.where(i == j, jnp.int32(v), out)
    return out


def kernel(q_hbm, k_hbm, v_hbm, o_hbm, do_hbm, lse_ref, dq_hbm, dk_hbm, dv_hbm,
           qb, dob, doall, oall, ld, kvb, acc, dqt, stage, nb, ub, fin, mine, dqs,
           loc, out_sem, sp, rp, ss, rk, sm, rn, sd, ru, se, re):
    s = lax.axis_index("seq")
    hd = lax.axis_index("heads")
    row = s // 4
    x = lax.rem(s, 4)
    pi = x // 2
    m = lax.rem(x, 2)
    mo = 1 - m
    g = jnp.where(pi == 0, m, mo)
    go = 1 - g
    sup = 2 * row + pi
    rows = lax.axis_size("seq") // 4

    def at_row(k):
        return lax.rem(row + k + rows, rows) * 4 + x

    partner = row * 4 + pi * 2 + mo
    nbr = row * 4 + 3 - x
    up1, up2, down1, down2 = at_row(1), at_row(2), at_row(-1), at_row(-2)

    def rc(src, dst, send, recv, dest):
        return pltpu.make_async_remote_copy(
            src_ref=src, dst_ref=dst, send_sem=send, recv_sem=recv,
            device_id=(hd, dest), device_id_type=pl.DeviceIdType.MESH)

    def cols(n, width):
        return pl.ds(pl.multiple_of(n * width, width), width)

    local = [
        pltpu.make_async_copy(k_hbm.at[:, cols(g, HEAD)], kvb.at[0, m, 0], loc.at[0]),
        pltpu.make_async_copy(v_hbm.at[:, cols(g, HEAD)], kvb.at[0, m, 1], loc.at[1]),
        pltpu.make_async_copy(do_hbm, doall, loc.at[2]),
        pltpu.make_async_copy(o_hbm, oall, loc.at[3]),
        pltpu.make_async_copy(q_hbm.at[:, cols(g, 4 * HEAD)], qb.at[0], loc.at[4]),
        pltpu.make_async_copy(do_hbm.at[:, cols(g, 4 * HEAD)], dob.at[0], loc.at[5]),
    ]
    for c in local:
        c.start()

    barrier = pltpu.get_barrier_semaphore()
    for d in (partner, nbr, up1, up2, down1, down2):
        pl.semaphore_signal(barrier, inc=1, device_id=(hd, d), device_id_type=pl.DeviceIdType.MESH)
    pl.semaphore_wait(barrier, 6)

    pair = [
        rc(k_hbm.at[:, cols(go, HEAD)], kvb.at[0, m, 0], sp.at[0], rp.at[0], partner),
        rc(v_hbm.at[:, cols(go, HEAD)], kvb.at[0, m, 1], sp.at[1], rp.at[1], partner),
        rc(do_hbm.at[:, cols(go, 4 * HEAD)], dob.at[1], sp.at[2], rp.at[2], partner),
        rc(q_hbm.at[:, cols(go, 4 * HEAD)], qb.at[1], sp.at[3], rp.at[3], partner),
    ]
    for c in pair:
        c.start()
    ld_copy = rc(ld.at[0], ld.at[1], sp.at[4], rp.at[4], partner)

    def to_up1(h):
        return rc(kvb.at[0, h], kvb.at[1, h], ss.at[0, h], rk.at[1, h], up1)

    def to_up2(h):
        return rc(kvb.at[0, h], kvb.at[2, h], ss.at[1, h], rk.at[2, h], up2)

    def forward(src, dst, h):
        return rc(kvb.at[src, h], kvb.at[dst, h], ss.at[dst - 1, h], rk.at[dst, h], nbr)

    def arrived(slot, h):
        rc(kvb.at[slot, h], kvb.at[slot, h], ss.at[0, h], rk.at[slot, h], nbr).wait_recv()

    def own_out(h):
        to_up1(h).start()
        to_up2(h).start()

        @pl.when(pi == 0)
        def _():
            forward(0, 3, h).start()

    local[0].wait()
    local[1].wait()
    own_out(m)

    ld[0, 0:8, :] = lse_ref[...] * LOG2E
    local[2].wait()
    local[3].wait()
    for h in range(8):
        c = slice(h * HEAD, (h + 1) * HEAD)
        prod = doall[:, c].astype(f32) * oall[:, c].astype(f32)
        ld[0, 8 + h:9 + h, :] = jnp.sum(prod.T, axis=0, keepdims=True)
    ld_copy.start()
    acc[...] = jnp.zeros_like(acc)
    dqt[...] = jnp.zeros_like(dqt)
    local[4].wait()
    local[5].wait()

    def tile(qs, slot, kh, h, k0, q0, qn, mask):
        hs = cols(h, HEAD)
        q = qb[qs, q0:q0 + qn, hs]
        do = dob[qs, q0:q0 + qn, hs]
        lse = ld[qs, pl.ds(g * 4 + h, 1), q0:q0 + qn]
        delta = ld[qs, pl.ds(8 + g * 4 + h, 1), q0:q0 + qn]
        k = kvb[slot, kh, 0, k0:k0 + 256, :]
        v = kvb[slot, kh, 1, k0:k0 + 256, :]
        p = jnp.exp2(dot(k, q, NT) * (SCALE * LOG2E) - lse)
        if mask is not None:
            kk = lax.broadcasted_iota(jnp.int32, p.shape, 0) + k0
            qq = lax.broadcasted_iota(jnp.int32, p.shape, 1) + q0
            p = jnp.where(qq >= kk if mask == "low" else kk > qq, p, 0.0)
        ds = (p * (dot(v, do, NT) - delta)).astype(bf16)
        acc[slot, kh, 1, k0:k0 + 256, :] += dot(p.astype(bf16), do, NN)
        acc[slot, kh, 0, k0:k0 + 256, :] += dot(ds, q, NN)
        dqt[qs, h, :, q0:q0 + qn] += dot(k, ds, TN)

    shapes = {
        "full": ((0, 0, 512, None), (256, 0, 512, None)),
        "low": ((0, 0, 512, "low"), (256, 256, 256, "low")),
        "up": ((0, 0, 256, "up"), (256, 0, 512, "up")),
    }

    def work(qs, slot, kh, kind):
        @pl.loop(0, 2)
        def _(h2):
            for u in range(2):
                for k0, q0, qn, mask in shapes[kind]:
                    tile(qs, slot, kh, h2 * 2 + u, k0, q0, qn, mask)

    def send_partial(slot, h, copy):
        stage[slot, h] = acc[slot, h].astype(bf16)
        copy.start()

    def to_nbr(n, h):
        return rc(stage.at[3 + n, h], nb.at[n, h], sm.at[n, h], rn.at[n, h], nbr)

    def to_down(n, h):
        return rc(stage.at[1 + n, h], ub.at[n, h], sd.at[n, h], ru.at[n, h], down1 if n == 0 else down2)

    def add_nbr(slot, n, h):
        rc(nb.at[n, h], nb.at[n, h], sm.at[n, h], rn.at[n, h], nbr).wait_recv()
        acc[slot, h] = acc[slot, h] + nb[n, h].astype(f32)

    @pl.loop(0, len(ITEMS))
    def _(i):
        qs = pick(i, [a for a, _, _ in ITEMS])
        slot = pick(i, [b for _, b, _ in ITEMS])
        par = pick(i, [c for _, _, c in ITEMS])
        back = pick(i, [BACK[b] for _, b, _ in ITEMS])
        kh = jnp.where(par == 0, m, mo)
        mq = jnp.where(qs == 0, m, mo)

        @pl.when(i == 1)
        def _():
            pair_in = rc(kvb.at[0, mo, 0], kvb.at[0, mo, 0], sp.at[0], rp.at[0], partner)
            pair_in.wait_recv()
            rc(kvb.at[0, mo, 1], kvb.at[0, mo, 1], sp.at[1], rp.at[1], partner).wait_recv()
            own_out(mo)

        @pl.when((i >= 2) & (i < 10))
        def _():
            arrived(slot, kh)

            @pl.when(slot == 1)
            def _():
                forward(1, 4 - pi, kh).start()

            @pl.when((slot == 2) & (pi == 1))
            def _():
                forward(2, 4, kh).start()

        @pl.when(i == 10)
        def _():
            pair[2].wait_recv()
            pair[3].wait_recv()
            ld_copy.wait_recv()

        gap = 2 * back + mq - kh
        valid = sup >= back

        @pl.when(valid & (gap > 0) & (gap < 8))
        def _():
            work(qs, slot, kh, "full")

        @pl.when(valid & (gap == 0))
        def _():
            work(qs, slot, kh, "low")

        @pl.when(valid & (gap == 8))
        def _():
            work(qs, slot, kh, "up")

        @pl.when((i >= 10) & (i < 14))
        def _():
            send_partial(slot, kh, to_nbr(slot - 3, kh))

        @pl.when((i >= 14) & (i < 16))
        def _():
            add_nbr(1, 1 - pi, kh)
            send_partial(1, kh, to_down(0, kh))

        @pl.when((i >= 16) & (i < 18))
        def _():
            @pl.when(pi == 1)
            def _():
                add_nbr(2, 1, kh)

            send_partial(2, kh, to_down(1, kh))

    def dq_stage(qs):
        for h in range(GROUP):
            dqs[qs, :, h * HEAD:(h + 1) * HEAD] = (dqt[qs, h] * SCALE).T.astype(bf16)

    dq_stage(1)
    dq_out = rc(dqs.at[1], dq_hbm.at[:, cols(g, 4 * HEAD)], se.at[0], re.at[0], partner)
    dq_out.start()
    dq_stage(0)
    dq_own = pltpu.make_async_copy(dqs.at[0], dq_hbm.at[:, cols(g, 4 * HEAD)], out_sem.at[0])
    dq_own.start()

    def finish(h, dst):
        @pl.when(pi == 0)
        def _():
            add_nbr(0, 0, h)

        for n in range(2):
            rc(ub.at[n, h], ub.at[n, h], sd.at[n, h], ru.at[n, h], up1).wait_recv()
        total = acc[0, h] + ub[0, h].astype(f32) + ub[1, h].astype(f32)
        dst[0] = (total[0] * SCALE).astype(bf16)
        dst[1] = total[1].astype(bf16)

    finish(mo, fin)
    ends = [
        rc(fin.at[0], dk_hbm.at[:, cols(g, HEAD)], se.at[1], re.at[1], partner),
        rc(fin.at[1], dv_hbm.at[:, cols(g, HEAD)], se.at[2], re.at[2], partner),
    ]
    for c in ends:
        c.start()
    finish(m, mine)
    outs = [
        pltpu.make_async_copy(mine.at[0], dk_hbm.at[:, cols(g, HEAD)], out_sem.at[1]),
        pltpu.make_async_copy(mine.at[1], dv_hbm.at[:, cols(g, HEAD)], out_sem.at[2]),
    ]
    for c in outs:
        c.start()

    for c in pair:
        c.wait_send()
    ld_copy.wait_send()
    for h in range(2):
        to_up1(h).wait_send()
        to_up2(h).wait_send()
        forward(0, 3, h).wait_send()
        forward(0, 4, h).wait_send()
        for n in range(2):
            to_nbr(n, h).wait_send()
            to_down(n, h).wait_send()
    rc(dqs.at[1], dq_hbm.at[:, cols(go, 4 * HEAD)], se.at[0], re.at[0], partner).wait()
    rc(fin.at[0], dk_hbm.at[:, cols(go, HEAD)], se.at[1], re.at[1], partner).wait()
    rc(fin.at[1], dv_hbm.at[:, cols(go, HEAD)], se.at[2], re.at[2], partner).wait()
    dq_own.wait()
    for c in outs:
        c.wait()


def shards(queries, keys, values, out, output_gradient, lse):
    hbm = pl.BlockSpec(memory_space=pl.ANY)
    vm = pl.BlockSpec(memory_space=pltpu.VMEM)
    dma = pltpu.SemaphoreType.DMA
    return pl.pallas_call(
        kernel,
        out_shape=(
            jax.ShapeDtypeStruct(queries.shape, bf16),
            jax.ShapeDtypeStruct(keys.shape, bf16),
            jax.ShapeDtypeStruct(values.shape, bf16),
        ),
        in_specs=[hbm] * 5 + [vm],
        out_specs=(hbm, hbm, hbm),
        scratch_shapes=[
            pltpu.VMEM((2, TOK, 4 * HEAD), bf16),
            pltpu.VMEM((2, TOK, 4 * HEAD), bf16),
            pltpu.VMEM((TOK, 8 * HEAD), bf16),
            pltpu.VMEM((TOK, 8 * HEAD), bf16),
            pltpu.VMEM((2, 16, TOK), f32),
            pltpu.VMEM((5, 2, 2, TOK, HEAD), bf16),
            pltpu.VMEM((5, 2, 2, TOK, HEAD), f32),
            pltpu.VMEM((2, GROUP, HEAD, TOK), f32),
            pltpu.VMEM((5, 2, 2, TOK, HEAD), bf16),
            pltpu.VMEM((2, 2, 2, TOK, HEAD), bf16),
            pltpu.VMEM((2, 2, 2, TOK, HEAD), bf16),
            pltpu.VMEM((2, TOK, HEAD), bf16),
            pltpu.VMEM((2, TOK, HEAD), bf16),
            pltpu.VMEM((2, TOK, 4 * HEAD), bf16),
            dma((6,)), dma((3,)), dma((5,)), dma((5,)),
            dma((4, 2)), dma((5, 2)),
            dma((2, 2)), dma((2, 2)), dma((2, 2)), dma((2, 2)),
            dma((3,)), dma((3,)),
        ],
        compiler_params=pltpu.CompilerParams(
            collective_id=0, has_side_effects=True, vmem_limit_bytes=48 << 20),
        name="swa_bwd",
    )(queries, keys, values, out, output_gradient, lse)


def solution(mesh):
    return jax.shard_map(
        shards,
        mesh=mesh,
        in_specs=(P("seq", "heads"),) * 5 + (P("heads", "seq"),),
        out_specs=(P("seq", "heads"),) * 3,
        check_vma=False,
    )
```

profile of v0, /device:TPU:32, one launch (start us, length us, event | category | flops | bytes accessed | tf_op | source)
XLA Modules:
  0.0 109.5 jit_solution(10035054930524670245)
XLA Ops:
  0.6 0.0 copy-start
  0.6 1.2 %copy-done = bf16[512,1024]{1,0:T(8,128)(2,1)S(1)} copy-done((bf16[512,1024]{1,0:T(8,128)(2,1)S(1)}, bf16[512,1024]{1,0:T(8,128)(2,1)}, u32[]{:S(2)}) %copy-start) | copy-done | bytes 1048600
  1.9 0.0 copy-start.1
  1.9 1.2 %copy-done.1 = bf16[512,1024]{1,0:T(8,128)(2,1)S(1)} copy-done((bf16[512,1024]{1,0:T(8,128)(2,1)S(1)}, bf16[512,1024]{1,0:T(8,128)(2,1)}, u32[]{:S(2)}) %copy-start.1) | copy-done | bytes 1048600
  3.1 0.0 copy-start.2
  3.1 1.2 %copy-done.2 = bf16[512,1024]{1,0:T(8,128)(2,1)S(1)} copy-done((bf16[512,1024]{1,0:T(8,128)(2,1)S(1)}, bf16[512,1024]{1,0:T(8,128)(2,1)}, u32[]{:S(2)}) %copy-start.2) | copy-done | bytes 1048600
  4.3 0.0 copy-start.3
  4.3 0.9 copy-done.3
  5.3 0.0 copy-start.4
  5.3 0.9 copy-done.4
  6.2 0.0 copy-start.5
  6.2 0.7 copy-done.5
  6.9 100.2 %swa_bwd.1 = (bf16[512,1024]{1,0:T(8,128)(2,1)S(1)}, bf16[512,256]{1,0:T(8,128)(2,1)S(1)}, bf16[512,256]{1,0:T(8,128)(2,1)S(1)}) custom-call(bf16[512,1024]{1,0:T(8,128)(2,1)S(1)} %copy-done, bf16[512,256]{1,0:T(8,128)(2,1)S(1)} %copy-done.3, bf16[512,256]{1,0:T(8,128)(2,1)S(1)} %copy-done.4, bf16[512,1024]{1,0:T(8,128)(2,1)S(1)} %copy-done.1, ...), custom_call_target="tpu_custom_call" | custom-call | tf_op jit(solution)/shard_map/swa_bwd/pallas_call | solution.py:305
  107.2 1.0 copy.12
  108.1 0.7 copy.13
  108.8 0.7 copy.14
Async XLA Ops:
  0.6 1.2 %copy-start = (bf16[512,1024]{1,0:T(8,128)(2,1)S(1)}, bf16[512,1024]{1,0:T(8,128)(2,1)}, u32[]{:S(2)}) copy-start(bf16[512,1024]{1,0:T(8,128)(2,1)} %q_hbm.1) | copy-start | bytes 3145732
  1.9 1.2 %copy-start.1 = (bf16[512,1024]{1,0:T(8,128)(2,1)S(1)}, bf16[512,1024]{1,0:T(8,128)(2,1)}, u32[]{:S(2)}) copy-start(bf16[512,1024]{1,0:T(8,128)(2,1)} %o_hbm.1) | copy-start | bytes 3145732
  3.1 1.2 %copy-start.2 = (bf16[512,1024]{1,0:T(8,128)(2,1)S(1)}, bf16[512,1024]{1,0:T(8,128)(2,1)}, u32[]{:S(2)}) copy-start(bf16[512,1024]{1,0:T(8,128)(2,1)} %do_hbm.1) | copy-start | bytes 3145732
  4.3 0.9 copy-start.3
  5.3 0.9 copy-start.4
  6.2 0.7 copy-start.5
where the time goes:
time: 110 us
  Pallas kernels  100 us (91%)
  local copies, waits for them, and re-layouts  8.66 us (8%)
    pallas_call x1, Pallas kernels, shards(): pl.pallas_call(kernel, out_shape=(jax.ShapeDtypeStruct(queries.shape, bf1...  100 us
    unnamed x15, local copies, waits for them, and re-layouts  8.66 us

commit v1 on v0

--- a/solution.py
+++ b/solution.py
@@ -19,10 +19,18 @@
 
 BACK = (0, 2, 4, 1, 3)
 ITEMS = (
-    (0, 0, 0), (0, 0, 1), (0, 1, 0), (0, 2, 0), (0, 1, 1), (0, 2, 1),
-    (0, 3, 1), (0, 3, 0), (0, 4, 1), (0, 4, 0),
-    (1, 3, 1), (1, 3, 0), (1, 4, 1), (1, 4, 0),
-    (1, 1, 0), (1, 1, 1), (1, 2, 0), (1, 2, 1), (1, 0, 1), (1, 0, 0),
+    (
+        (0, 0, 0), (0, 0, 1), (0, 1, 0), (0, 2, 0), (0, 1, 1),
+        (0, 3, 1), (0, 2, 1), (0, 3, 0), (0, 4, 1), (0, 4, 0),
+        (1, 3, 0), (1, 3, 1), (1, 4, 0), (1, 4, 1), (1, 2, 1),
+        (1, 2, 0), (1, 1, 1), (1, 1, 0), (1, 0, 1), (1, 0, 0),
+    ),
+    (
+        (0, 0, 0), (0, 0, 1), (0, 3, 1), (0, 1, 0), (0, 2, 0),
+        (0, 3, 0), (0, 1, 1), (0, 2, 1), (0, 4, 1), (0, 4, 0),
+        (1, 4, 0), (1, 4, 1), (1, 3, 0), (1, 3, 1), (1, 1, 1),
+        (1, 1, 0), (1, 2, 1), (1, 2, 0), (1, 0, 1), (1, 0, 0),
+    ),
 )
 
 
@@ -176,12 +184,14 @@
         rc(nb.at[n, h], nb.at[n, h], sm.at[n, h], rn.at[n, h], nbr).wait_recv()
         acc[slot, h] = acc[slot, h] + nb[n, h].astype(f32)
 
-    @pl.loop(0, len(ITEMS))
+    @pl.loop(0, 20)
     def _(i):
-        qs = pick(i, [a for a, _, _ in ITEMS])
-        slot = pick(i, [b for _, b, _ in ITEMS])
-        par = pick(i, [c for _, _, c in ITEMS])
-        back = pick(i, [BACK[b] for _, b, _ in ITEMS])
+        at = i + 20 * pi
+        items = ITEMS[0] + ITEMS[1]
+        qs = pick(at, [a for a, _, _ in items])
+        slot = pick(at, [b for _, b, _ in items])
+        par = pick(at, [c for _, _, c in items])
+        back = pick(slot, BACK)
         kh = jnp.where(par == 0, m, mo)
         mq = jnp.where(qs == 0, m, mo)
 
@@ -225,21 +235,17 @@
         def _():
             work(qs, slot, kh, "up")
 
-        @pl.when((i >= 10) & (i < 14))
+        @pl.when((qs == 1) & (slot >= 3))
         def _():
             send_partial(slot, kh, to_nbr(slot - 3, kh))
 
-        @pl.when((i >= 14) & (i < 16))
+        @pl.when((qs == 1) & (slot == 1))
         def _():
             add_nbr(1, 1 - pi, kh)
             send_partial(1, kh, to_down(0, kh))
 
-        @pl.when((i >= 16) & (i < 18))
-        def _():
-            @pl.when(pi == 1)
-            def _():
-                add_nbr(2, 1, kh)
-
+        @pl.when((qs == 1) & (slot == 2) & (pi == 0))
+        def _():
             send_partial(2, kh, to_down(1, kh))
 
     def dq_stage(qs):
@@ -249,6 +255,13 @@
     dq_stage(1)
     dq_out = rc(dqs.at[1], dq_hbm.at[:, cols(g, 4 * HEAD)], se.at[0], re.at[0], partner)
     dq_out.start()
+
+    @pl.when(pi == 1)
+    def _():
+        for h in (mo, m):
+            add_nbr(2, 1, h)
+            send_partial(2, h, to_down(1, h))
+
     dq_stage(0)
     dq_own = pltpu.make_async_copy(dqs.at[0], dq_hbm.at[:, cols(g, 4 * HEAD)], out_sem.at[0])
     dq_own.start()

time: 110 us -> 103 us (0.936)
  Pallas kernels: 100 us -> 92.7 us
    pallas_call x1, Pallas kernels: 100 us -> 92.7 us  [shards(): pl.pallas_call(kernel, out_shape=(jax.ShapeDtypeStruct(queries.shape, bf1...]
where the time goes in v1:
time: 103 us; the launch traced here: 102 us
  Pallas kernels  92.7 us (90%)
  local copies, waits for them, and re-layouts  8.66 us (8%)
    pallas_call x1, Pallas kernels, shards(): pl.pallas_call(kernel, out_shape=(jax.ShapeDtypeStruct(queries.shape, bf1...  92.7 us
    unnamed x15, local copies, waits for them, and re-layouts  8.66 us

profile of v1, /device:TPU:32, one launch (start us, length us, event | category | flops | bytes accessed | tf_op | source)
XLA Modules:
  0.0 102.1 jit_solution(4682066157590050484)
XLA Ops:
  0.6 0.0 copy-start
  0.6 1.2 %copy-done = bf16[512,1024]{1,0:T(8,128)(2,1)S(1)} copy-done((bf16[512,1024]{1,0:T(8,128)(2,1)S(1)}, bf16[512,1024]{1,0:T(8,128)(2,1)}, u32[]{:S(2)}) %copy-start) | copy-done | bytes 1048600
  1.9 0.0 copy-start.1
  1.9 1.2 %copy-done.1 = bf16[512,1024]{1,0:T(8,128)(2,1)S(1)} copy-done((bf16[512,1024]{1,0:T(8,128)(2,1)S(1)}, bf16[512,1024]{1,0:T(8,128)(2,1)}, u32[]{:S(2)}) %copy-start.1) | copy-done | bytes 1048600
  3.1 0.0 copy-start.2
  3.1 1.2 %copy-done.2 = bf16[512,1024]{1,0:T(8,128)(2,1)S(1)} copy-done((bf16[512,1024]{1,0:T(8,128)(2,1)S(1)}, bf16[512,1024]{1,0:T(8,128)(2,1)}, u32[]{:S(2)}) %copy-start.2) | copy-done | bytes 1048600
  4.3 0.0 copy-start.3
  4.3 0.9 copy-done.3
  5.3 0.0 copy-start.4
  5.3 0.9 copy-done.4
  6.2 0.0 copy-start.5
  6.2 0.7 copy-done.5
  6.9 92.7 %swa_bwd.1 = (bf16[512,1024]{1,0:T(8,128)(2,1)S(1)}, bf16[512,256]{1,0:T(8,128)(2,1)S(1)}, bf16[512,256]{1,0:T(8,128)(2,1)S(1)}) custom-call(bf16[512,1024]{1,0:T(8,128)(2,1)S(1)} %copy-done, bf16[512,256]{1,0:T(8,128)(2,1)S(1)} %copy-done.3, bf16[512,256]{1,0:T(8,128)(2,1)S(1)} %copy-done.4, bf16[512,1024]{1,0:T(8,128)(2,1)S(1)} %copy-done.1, ...), custom_call_target="tpu_custom_call" | custom-call | tf_op jit(solution)/shard_map/swa_bwd/pallas_call | solution.py:318
  99.7 1.0 copy.12
  100.7 0.7 copy.13
  101.4 0.7 copy.14
Async XLA Ops:
  0.6 1.2 %copy-start = (bf16[512,1024]{1,0:T(8,128)(2,1)S(1)}, bf16[512,1024]{1,0:T(8,128)(2,1)}, u32[]{:S(2)}) copy-start(bf16[512,1024]{1,0:T(8,128)(2,1)} %q_hbm.1) | copy-start | bytes 3145732
  1.9 1.2 %copy-start.1 = (bf16[512,1024]{1,0:T(8,128)(2,1)S(1)}, bf16[512,1024]{1,0:T(8,128)(2,1)}, u32[]{:S(2)}) copy-start(bf16[512,1024]{1,0:T(8,128)(2,1)} %o_hbm.1) | copy-start | bytes 3145732
  3.1 1.2 %copy-start.2 = (bf16[512,1024]{1,0:T(8,128)(2,1)S(1)}, bf16[512,1024]{1,0:T(8,128)(2,1)}, u32[]{:S(2)}) copy-start(bf16[512,1024]{1,0:T(8,128)(2,1)} %do_hbm.1) | copy-start | bytes 3145732
  4.3 0.9 copy-start.3
  5.3 0.9 copy-start.4
  6.2 0.7 copy-start.5

commit v2 on v1

--- a/solution.py
+++ b/solution.py
@@ -20,14 +20,14 @@
 BACK = (0, 2, 4, 1, 3)
 ITEMS = (
     (
-        (0, 0, 0), (0, 0, 1), (0, 1, 0), (0, 2, 0), (0, 1, 1),
-        (0, 3, 1), (0, 2, 1), (0, 3, 0), (0, 4, 1), (0, 4, 0),
+        (0, 0, 0), (0, 0, 1), (0, 2, 0), (0, 1, 0), (0, 2, 1),
+        (0, 1, 1), (0, 3, 1), (0, 3, 0), (0, 4, 1), (0, 4, 0),
         (1, 3, 0), (1, 3, 1), (1, 4, 0), (1, 4, 1), (1, 2, 1),
         (1, 2, 0), (1, 1, 1), (1, 1, 0), (1, 0, 1), (1, 0, 0),
     ),
     (
-        (0, 0, 0), (0, 0, 1), (0, 3, 1), (0, 1, 0), (0, 2, 0),
-        (0, 3, 0), (0, 1, 1), (0, 2, 1), (0, 4, 1), (0, 4, 0),
+        (0, 0, 0), (0, 0, 1), (0, 3, 1), (0, 2, 0), (0, 1, 0),
+        (0, 2, 1), (0, 1, 1), (0, 3, 0), (0, 4, 1), (0, 4, 0),
         (1, 4, 0), (1, 4, 1), (1, 3, 0), (1, 3, 1), (1, 1, 1),
         (1, 1, 0), (1, 2, 1), (1, 2, 0), (1, 0, 1), (1, 0, 0),
     ),
@@ -114,9 +114,15 @@
     def arrived(slot, h):
         rc(kvb.at[slot, h], kvb.at[slot, h], ss.at[0, h], rk.at[slot, h], nbr).wait_recv()
 
+    def relay(h):
+        return rc(kvb.at[2, h], kvb.at[1, h], ss.at[0, h], rk.at[1, h], down1)
+
     def own_out(h):
-        to_up1(h).start()
         to_up2(h).start()
+
+        @pl.when(lax.rem(row, 2) == 0)
+        def _():
+            to_up1(h).start()
 
         @pl.when(pi == 0)
         def _():
@@ -195,7 +201,7 @@
         kh = jnp.where(par == 0, m, mo)
         mq = jnp.where(qs == 0, m, mo)
 
-        @pl.when(i == 1)
+        @pl.when(i == 0)
         def _():
             pair_in = rc(kvb.at[0, mo, 0], kvb.at[0, mo, 0], sp.at[0], rp.at[0], partner)
             pair_in.wait_recv()
@@ -205,6 +211,10 @@
         @pl.when((i >= 2) & (i < 10))
         def _():
             arrived(slot, kh)
+
+            @pl.when((slot == 2) & (lax.rem(row, 2) == 1))
+            def _():
+                relay(kh).start()
 
             @pl.when(slot == 1)
             def _():

time: 103 us -> 106 us (1.029); the launches traced: 102 us -> 104 us
  Pallas kernels: 92.7 us -> 94.4 us
    pallas_call x1, Pallas kernels: 92.7 us -> 94.4 us  [shards(): pl.pallas_call(kernel, out_shape=(jax.ShapeDtypeStruct(queries.shape, bf1...]
where the time goes in v2:
time: 106 us; the launch traced here: 104 us
  Pallas kernels  94.4 us (89%)
  local copies, waits for them, and re-layouts  8.66 us (8%)
    pallas_call x1, Pallas kernels, shards(): pl.pallas_call(kernel, out_shape=(jax.ShapeDtypeStruct(queries.shape, bf1...  94.4 us
    unnamed x15, local copies, waits for them, and re-layouts  8.66 us

profile of v2, /device:TPU:32, one launch (start us, length us, event | category | flops | bytes accessed | tf_op | source)
XLA Modules:
  0.0 103.7 jit_solution(15449088769633084695)
XLA Ops:
  0.6 0.0 copy-start
  0.6 1.2 %copy-done = bf16[512,1024]{1,0:T(8,128)(2,1)S(1)} copy-done((bf16[512,1024]{1,0:T(8,128)(2,1)S(1)}, bf16[512,1024]{1,0:T(8,128)(2,1)}, u32[]{:S(2)}) %copy-start) | copy-done | bytes 1048600
  1.9 0.0 copy-start.1
  1.9 1.2 %copy-done.1 = bf16[512,1024]{1,0:T(8,128)(2,1)S(1)} copy-done((bf16[512,1024]{1,0:T(8,128)(2,1)S(1)}, bf16[512,1024]{1,0:T(8,128)(2,1)}, u32[]{:S(2)}) %copy-start.1) | copy-done | bytes 1048600
  3.1 0.0 copy-start.2
  3.1 1.2 %copy-done.2 = bf16[512,1024]{1,0:T(8,128)(2,1)S(1)} copy-done((bf16[512,1024]{1,0:T(8,128)(2,1)S(1)}, bf16[512,1024]{1,0:T(8,128)(2,1)}, u32[]{:S(2)}) %copy-start.2) | copy-done | bytes 1048600
  4.3 0.0 copy-start.3
  4.3 0.9 copy-done.3
  5.3 0.0 copy-start.4
  5.3 0.9 copy-done.4
  6.2 0.0 copy-start.5
  6.2 0.7 copy-done.5
  6.9 94.4 %swa_bwd.1 = (bf16[512,1024]{1,0:T(8,128)(2,1)S(1)}, bf16[512,256]{1,0:T(8,128)(2,1)S(1)}, bf16[512,256]{1,0:T(8,128)(2,1)S(1)}) custom-call(bf16[512,1024]{1,0:T(8,128)(2,1)S(1)} %copy-done, bf16[512,256]{1,0:T(8,128)(2,1)S(1)} %copy-done.3, bf16[512,256]{1,0:T(8,128)(2,1)S(1)} %copy-done.4, bf16[512,1024]{1,0:T(8,128)(2,1)S(1)} %copy-done.1, ...), custom_call_target="tpu_custom_call" | custom-call | tf_op jit(solution)/shard_map/swa_bwd/pallas_call | solution.py:328
  101.3 1.0 copy.12
  102.3 0.7 copy.13
  103.0 0.7 copy.14
Async XLA Ops:
  0.6 1.2 %copy-start = (bf16[512,1024]{1,0:T(8,128)(2,1)S(1)}, bf16[512,1024]{1,0:T(8,128)(2,1)}, u32[]{:S(2)}) copy-start(bf16[512,1024]{1,0:T(8,128)(2,1)} %q_hbm.1) | copy-start | bytes 3145732
  1.9 1.2 %copy-start.1 = (bf16[512,1024]{1,0:T(8,128)(2,1)S(1)}, bf16[512,1024]{1,0:T(8,128)(2,1)}, u32[]{:S(2)}) copy-start(bf16[512,1024]{1,0:T(8,128)(2,1)} %o_hbm.1) | copy-start | bytes 3145732
  3.1 1.2 %copy-start.2 = (bf16[512,1024]{1,0:T(8,128)(2,1)S(1)}, bf16[512,1024]{1,0:T(8,128)(2,1)}, u32[]{:S(2)}) copy-start(bf16[512,1024]{1,0:T(8,128)(2,1)} %do_hbm.1) | copy-start | bytes 3145732
  4.3 0.9 copy-start.3
  5.3 0.9 copy-start.4
  6.2 0.7 copy-start.5
